TPU v7x, 512 devices: a whole 4x8x8 slice. The times are simulated.
512 devices in a mesh: cache: 64 (over x, z, core), rank: 8 (over y).
Axes of the slice: x: 4, y: 8, z: 8, core: 2. Of those that a mesh axis runs over, the one named last changes fastest.
Arguments:
- cand_rows: bfloat16 [64, 64, 4, 1024], P('cache', None, None, 'rank'), may hold values from -48 to 48
- listed: int32 [64], replicated, may hold values from 0 to 63, each once
- hist_len: int32 [64], P('cache'), may hold values from 768 to 3072, as said below
- block_mask: int32 [64, 24], P('cache'), may hold values 0 or 1
- hist_keys: bfloat16 [1, 64, 3072, 1024], P(None, 'cache', None, 'rank'), may hold values from -6 to 6
- hist_values: bfloat16 [1, 64, 3072, 1024], P(None, 'cache', None, 'rank'), may hold values from -6 to 6
- w_query: bfloat16 [1, 1024, 1024], P(None, None, 'rank'), may hold values from -0.1875 to 0.1875
- w_gate: bfloat16 [1, 1024, 1024], P(None, None, 'rank'), may hold values from -0.1875 to 0.1875
- w_out: bfloat16 [1, 1024, 1024], P(None, None, 'rank'), may hold values from -0.1875 to 0.1875
Outputs:
- ranked: bfloat16 [64, 64, 4, 1024], P('cache', None, None, 'rank')
Inputs may be any that keep to these rules, and one draw needn't show every extreme that they name: `hist_len`: some user has exactly 3072 history events. `listed`: each user id appears once.
All inputs are finite; a program needn't handle non-finite values. No bound on the sum of `block_mask` on one device may be relied on, other than what follows from the above.
Results may differ from a plain program's by a relative error of at most 0.0024.
Values may be sent and summed in bfloat16 or wider, within the bound.
A program may use at most 64 MiB of HBM per device.

v0:
```python
import jax
import jax.numpy as jnp
from jax import lax
from jax.sharding import PartitionSpec as P

D = 1024
HEADS = 8
BLOCK = 128


EPSILON = 1e-05
GROUP_BLOCKS = 4


def head_norm(values):
    centre = jnp.mean(values, axis=-1, keepdims=True)
    spread = jnp.mean(jnp.square(values - centre), axis=-1, keepdims=True)
    return (values - centre) * lax.rsqrt(spread + EPSILON)


def attend(queries, key_cache, value_cache, length, block_list, block_live, turn_count):
    head_size = queries.shape[-1]
    score_scale = head_size ** (-0.5)
    within = jnp.arange(BLOCK, dtype=jnp.int32)
    running = jnp.zeros(queries.shape, jnp.float32)

    def one_turn(turn_no, running):
        chosen = lax.dynamic_slice_in_dim(block_list, turn_no * GROUP_BLOCKS, GROUP_BLOCKS)
        chosen_live = lax.dynamic_slice_in_dim(block_live, turn_no * GROUP_BLOCKS, GROUP_BLOCKS)
        key_rows = jnp.take(key_cache, chosen, axis=0).reshape(
            GROUP_BLOCKS * BLOCK, key_cache.shape[2], head_size
        )
        value_rows = jnp.take(value_cache, chosen, axis=0).reshape(
            GROUP_BLOCKS * BLOCK, key_cache.shape[2], head_size
        )
        places = (chosen[:, None] * BLOCK + within[None, :]).reshape(GROUP_BLOCKS * BLOCK)
        live_mask = ((places < length) & jnp.repeat(chosen_live, BLOCK)).astype(jnp.float32)
        scores = (
            jnp.einsum("nkhe,the->nkht", queries, key_rows, preferred_element_type=jnp.float32)
            * score_scale
        )
        weights = (jax.nn.silu(scores) * live_mask).astype(jnp.bfloat16)
        return running + jnp.einsum(
            "nkht,the->nkhe", weights, value_rows, preferred_element_type=jnp.float32
        )

    return lax.fori_loop(0, turn_count, one_turn, running)


def finish(result):
    return lax.all_to_all(result, "cache", split_axis=0, concat_axis=1, tiled=True)


def on_device(
    cand_rows, listed, hist_len, block_mask, hist_keys, hist_values, w_query, w_gate, w_out
):
    head_size = D // HEADS
    local_width = w_query.shape[2]
    local_heads = local_width // head_size
    blocks_total = block_mask.shape[1]
    padded = -(-blocks_total // GROUP_BLOCKS) * GROUP_BLOCKS
    slot_of_user = jnp.argsort(listed)
    outgoing = jnp.take(cand_rows, slot_of_user, axis=1)
    length = hist_len[0]
    starts = jnp.arange(blocks_total, dtype=jnp.int32) * BLOCK
    usable = (block_mask[0] == 1) & (starts < length)
    filler = jnp.zeros((padded - blocks_total,), jnp.int32)
    block_list = jnp.concatenate([jnp.arange(blocks_total, dtype=jnp.int32), filler])
    block_live = jnp.concatenate([usable, filler > 0])
    turn_count = padded // GROUP_BLOCKS
    current = lax.all_to_all(outgoing, "cache", split_axis=1, concat_axis=0, tiled=True)
    whole_rows = lax.all_gather(current, "rank", axis=3, tiled=True)
    normed = head_norm(whole_rows.astype(jnp.float32)).astype(jnp.bfloat16)
    queries = jax.nn.silu(
        jnp.einsum("nukd,de->nuke", normed, w_query[0], preferred_element_type=jnp.float32)
    ).astype(jnp.bfloat16)
    gate_act = jax.nn.silu(
        jnp.einsum("nukd,de->nuke", normed, w_gate[0], preferred_element_type=jnp.float32)
    )
    split_shape = queries.shape[:3] + (local_heads, head_size)
    queries = queries.reshape(split_shape)
    length, block_list, block_live, turn_count = (length, block_list, block_live, turn_count)
    key_cache = hist_keys[0, 0].reshape(blocks_total, BLOCK, local_heads, head_size)
    value_cache = hist_values[0, 0].reshape(blocks_total, BLOCK, local_heads, head_size)
    attended_list = [
        attend(queries[:, 0], key_cache, value_cache, length, block_list, block_live, turn_count)
    ]
    attended = jnp.stack(attended_list, axis=1)
    hidden = (
        (head_norm(attended) * gate_act.reshape(split_shape))
        .reshape(queries.shape[:3] + (local_width,))
        .astype(jnp.bfloat16)
    )
    rows_in = w_out[0]
    projected = jnp.einsum(
        "nukd,de->nuke",
        lax.all_gather(hidden, "rank", axis=3, tiled=True),
        rows_in,
        preferred_element_type=jnp.float32,
    )
    current = (current.astype(jnp.float32) + projected).astype(jnp.bfloat16)
    returned = finish(current)
    return jnp.take(returned, listed, axis=1)


def solution(mesh):
    placed = (
        P("cache", None, None, "rank"),
        P(),
        P("cache"),
        P("cache", None),
        P(None, "cache", None, "rank"),
        P(None, "cache", None, "rank"),
        P(None, None, "rank"),
        P(None, None, "rank"),
        P(None, None, "rank"),
    )
    return jax.shard_map(
        on_device,
        mesh=mesh,
        in_specs=placed,
        out_specs=P("cache", None, None, "rank"),
        check_vma=False,
    )
```

profile of v0, /device:TPU:1, one launch (start us, length us, event | category | flops | bytes accessed | tf_op | source)
XLA Modules:
  0.0 122.2 jit_solution(12769290152046905703)
XLA Ops:
  0.7 2.0 %sort.17 = (s32[64]{0:T(128)}, s32[64]{0:T(128)S(1)}) sort(s32[64]{0:T(128)S(1)} %copy-done.4, s32[64]{0:T(128)S(1)} %iota.13), dimensions={0}, to_apply=%region_0.0 | sort | flops 384 | bytes 1024 | tf_op jit(solution)/shard_map/jit(argsort)/sort | solution.py:62
  2.8 1.5 %gather_fusion.2 = bf16[64,4,128]{2,1,0:T(4,128)(2,1)S(1)} fusion(bf16[64,4,128]{2,1,0:T(4,128)(2,1)} %bitcast.138, s32[1024]{0:T(1024)S(1)} %pad_clamp_fusion.2), kind=kCustom, calls=%fused_computation.clone | custom fusion | bytes 131328 | tf_op jit(solution)/shard_map/jit(_take)/gather | solution.py:63
  4.3 0.8 fusion.45
  5.0 14.8 %all-to-all-start = ((bf16[1,64,4,128]{3,2,0,1:T(4,128)(2,1)}), bf16[1,64,4,128]{3,2,0,1:T(4,128)(2,1)S(1)}, u32[]{:S(2)}, u32[]{:S(2)}) async-start(bf16[1,64,4,128]{3,2,0,1:T(4,128)(2,1)} %fusion.45), calls=%async_computation | async-start | bytes 131072 | tf_op jit(solution)/shard_map/all_to_all | solution.py:71
  21.2 8.5 %all-to-all-done = bf16[1,64,4,128]{3,2,0,1:T(4,128)(2,1)S(1)} async-done(((bf16[1,64,4,128]{3,2,0,1:T(4,128)(2,1)}), bf16[1,64,4,128]{3,2,0,1:T(4,128)(2,1)S(1)}, u32[]{:S(2)}, u32[]{:S(2)}) %all-to-all-start) | async-done | bytes 65568 | tf_op jit(solution)/shard_map/all_to_all | solution.py:71
  29.7 15.8 %all-gather = bf16[1,64,4,1024]{3,2,0,1:T(4,128)(2,1)S(1)} all-gather(bf16[1,64,4,128]{3,2,0,1:T(4,128)(2,1)S(1)} %all-to-all-done), channel_id=2, replica_groups=mesh['cache'=64,'rank'=8] {'rank'}, dimensions={3}, use_global_device_ids=true | all-gather | bytes 589824 | tf_op jit(solution)/shard_map/all_gather | solution.py:72
  47.0 29.7 %while.14 = (s32[]{:T(128)}, f32[64,4,1,128]{3,0,1,2:T(8,128)S(1)}, s32[24]{0:T(128)S(1)}, bf16[24,128,1,128]{3,1,0,2:T(8,128)(2,1)}, bf16[24,128,1,128]{3,1,0,2...) while((s32[]{:T(128)}, f32[64,4,1,128]{3,0,1,2:T(8,128)S(1)}, ...), condition=%wide.region_4.7_spmd.clone, body=%wide.region_3.6_spmd.clone.sunk | while | flops 68226080 | bytes 1646929 | solution.py:47
  47.1 1.7 %gather_fusion = bf16[4,128,128]{2,1,0:T(8,128)(2,1)S(1)} fusion(bf16[24,128,128]{2,1,0:T(8,128)(2,1)} %bitcast.136, s32[1024]{0:T(1024)S(1)} %pad_clamp_fusion.4), kind=kCustom, calls=%fused_computation.3.clone.clone.1 | custom fusion | bytes 262160 | tf_op jit(solution)/shard_map/while/body/eval_jaxpr/jit(_take)/gather | solution.py:30
  48.8 1.7 %gather_fusion.1 = bf16[4,128,128]{2,1,0:T(8,128)(2,1)S(1)} fusion(bf16[24,128,128]{2,1,0:T(8,128)(2,1)} %bitcast.134, s32[1024]{0:T(1024)S(1)} %pad_clamp_fusion.4), kind=kCustom, calls=%fused_computation.1.clone.clone.1 | custom fusion | bytes 262160 | tf_op jit(solution)/shard_map/while/body/eval_jaxpr/jit(_take)/gather | solution.py:33
  50.7 0.7 convert_bitcast_fusion.3
  52.0 1.7 %gather_fusion = bf16[4,128,128]{2,1,0:T(8,128)(2,1)S(1)} fusion(bf16[24,128,128]{2,1,0:T(8,128)(2,1)} %bitcast.136, s32[1024]{0:T(1024)S(1)} %pad_clamp_fusion.4), kind=kCustom, calls=%fused_computation.3.clone.clone.1 | custom fusion | bytes 262160 | tf_op jit(solution)/shard_map/while/body/eval_jaxpr/jit(_take)/gather | solution.py:30
  53.7 1.7 %gather_fusion.1 = bf16[4,128,128]{2,1,0:T(8,128)(2,1)S(1)} fusion(bf16[24,128,128]{2,1,0:T(8,128)(2,1)} %bitcast.134, s32[1024]{0:T(1024)S(1)} %pad_clamp_fusion.4), kind=kCustom, calls=%fused_computation.1.clone.clone.1 | custom fusion | bytes 262160 | tf_op jit(solution)/shard_map/while/body/eval_jaxpr/jit(_take)/gather | solution.py:33
  57.0 1.7 %gather_fusion = bf16[4,128,128]{2,1,0:T(8,128)(2,1)S(1)} fusion(bf16[24,128,128]{2,1,0:T(8,128)(2,1)} %bitcast.136, s32[1024]{0:T(1024)S(1)} %pad_clamp_fusion.4), kind=kCustom, calls=%fused_computation.3.clone.clone.1 | custom fusion | bytes 262160 | tf_op jit(solution)/shard_map/while/body/eval_jaxpr/jit(_take)/gather | solution.py:30
  58.7 1.7 %gather_fusion.1 = bf16[4,128,128]{2,1,0:T(8,128)(2,1)S(1)} fusion(bf16[24,128,128]{2,1,0:T(8,128)(2,1)} %bitcast.134, s32[1024]{0:T(1024)S(1)} %pad_clamp_fusion.4), kind=kCustom, calls=%fused_computation.1.clone.clone.1 | custom fusion | bytes 262160 | tf_op jit(solution)/shard_map/while/body/eval_jaxpr/jit(_take)/gather | solution.py:33
  61.9 1.7 %gather_fusion = bf16[4,128,128]{2,1,0:T(8,128)(2,1)S(1)} fusion(bf16[24,128,128]{2,1,0:T(8,128)(2,1)} %bitcast.136, s32[1024]{0:T(1024)S(1)} %pad_clamp_fusion.4), kind=kCustom, calls=%fused_computation.3.clone.clone.1 | custom fusion | bytes 262160 | tf_op jit(solution)/shard_map/while/body/eval_jaxpr/jit(_take)/gather | solution.py:30
  63.6 1.7 %gather_fusion.1 = bf16[4,128,128]{2,1,0:T(8,128)(2,1)S(1)} fusion(bf16[24,128,128]{2,1,0:T(8,128)(2,1)} %bitcast.134, s32[1024]{0:T(1024)S(1)} %pad_clamp_fusion.4), kind=kCustom, calls=%fused_computation.1.clone.clone.1 | custom fusion | bytes 262160 | tf_op jit(solution)/shard_map/while/body/eval_jaxpr/jit(_take)/gather | solution.py:33
  66.9 1.7 %gather_fusion = bf16[4,128,128]{2,1,0:T(8,128)(2,1)S(1)} fusion(bf16[24,128,128]{2,1,0:T(8,128)(2,1)} %bitcast.136, s32[1024]{0:T(1024)S(1)} %pad_clamp_fusion.4), kind=kCustom, calls=%fused_computation.3.clone.clone.1 | custom fusion | bytes 262160 | tf_op jit(solution)/shard_map/while/body/eval_jaxpr/jit(_take)/gather | solution.py:30
  68.6 1.7 %gather_fusion.1 = bf16[4,128,128]{2,1,0:T(8,128)(2,1)S(1)} fusion(bf16[24,128,128]{2,1,0:T(8,128)(2,1)} %bitcast.134, s32[1024]{0:T(1024)S(1)} %pad_clamp_fusion.4), kind=kCustom, calls=%fused_computation.1.clone.clone.1 | custom fusion | bytes 262160 | tf_op jit(solution)/shard_map/while/body/eval_jaxpr/jit(_take)/gather | solution.py:33
  71.8 1.7 %gather_fusion = bf16[4,128,128]{2,1,0:T(8,128)(2,1)S(1)} fusion(bf16[24,128,128]{2,1,0:T(8,128)(2,1)} %bitcast.136, s32[1024]{0:T(1024)S(1)} %pad_clamp_fusion.4), kind=kCustom, calls=%fused_computation.3.clone.clone.1 | custom fusion | bytes 262160 | tf_op jit(solution)/shard_map/while/body/eval_jaxpr/jit(_take)/gather | solution.py:30
  73.6 1.7 %gather_fusion.1 = bf16[4,128,128]{2,1,0:T(8,128)(2,1)S(1)} fusion(bf16[24,128,128]{2,1,0:T(8,128)(2,1)} %bitcast.134, s32[1024]{0:T(1024)S(1)} %pad_clamp_fusion.4), kind=kCustom, calls=%fused_computation.1.clone.clone.1 | custom fusion | bytes 262160 | tf_op jit(solution)/shard_map/while/body/eval_jaxpr/jit(_take)/gather | solution.py:33
  78.0 19.5 %all-gather.1 = bf16[64,4,1024]{2,0,1:T(8,128)(2,1)S(1)} all-gather(bf16[64,4,128]{2,0,1:T(8,128)(2,1)S(1)} %fusion.31), channel_id=3, replica_groups=mesh['cache'=64,'rank'=8] {'rank'}, dimensions={2}, use_global_device_ids=true | all-gather | bytes 589824 | tf_op jit(solution)/shard_map/all_gather | solution.py:97
  98.5 12.4 %all-to-all-start.1 = ((bf16[64,1,4,128]{3,2,1,0:T(4,128)(2,1)}), bf16[64,1,4,128]{3,2,1,0:T(4,128)(2,1)S(1)}, u32[]{:S(2)}, u32[]{:S(2)}) async-start(bf16[64,1,4,128]{3,2,1,0:T(4,128)(2,1)} %copy.46), calls=%async_computation.1 | async-start | bytes 131072 | tf_op jit(solution)/shard_map/all_to_all | solution.py:51
  110.9 9.9 %all-to-all-done.1 = bf16[64,1,4,128]{3,2,1,0:T(4,128)(2,1)S(1)} async-done(((bf16[64,1,4,128]{3,2,1,0:T(4,128)(2,1)}), bf16[64,1,4,128]{3,2,1,0:T(4,128)(2,1)S(1)}, u32[]{:S(2)}, u32[]{:S(2)}) %all-to-all-start.1) | async-done | bytes 65568 | tf_op jit(solution)/shard_map/all_to_all | solution.py:51
  121.4 0.8 bitcast_select_fusion.2
  (75 shorter events, 14.0 us)
Async XLA Ops:
  0.0 46.6 %copy-start = (bf16[1,1024,128]{2,1,0:T(8,128)(2,1)S(1)}, bf16[1,1024,128]{2,1,0:T(8,128)(2,1)}, u32[]{:S(2)}) copy-start(bf16[1,1024,128]{2,1,0:T(8,128)(2,1)} %param.21) | copy-start | bytes 786436
  0.0 0.7 copy-start.4
  5.0 24.6 %all-to-all-start = ((bf16[1,64,4,128]{3,2,0,1:T(4,128)(2,1)}), bf16[1,64,4,128]{3,2,0,1:T(4,128)(2,1)S(1)}, u32[]{:S(2)}, u32[]{:S(2)}) async-start(bf16[1,64,4,128]{3,2,0,1:T(4,128)(2,1)} %fusion.45), calls=%async_computation | async-start | bytes 131072 | tf_op jit(solution)/shard_map/all_to_all | solution.py:71
  20.5 0.7 copy-start.3
  76.7 1.0 copy-start.2
  78.0 19.5 %copy-start.1 = (bf16[1,1024,128]{2,1,0:T(8,128)(2,1)S(1)}, bf16[1,1024,128]{2,1,0:T(8,128)(2,1)}, u32[]{:S(2)}) copy-start(bf16[1,1024,128]{2,1,0:T(8,128)(2,1)} %param.23) | copy-start | bytes 786436
  98.5 22.3 %all-to-all-start.1 = ((bf16[64,1,4,128]{3,2,1,0:T(4,128)(2,1)}), bf16[64,1,4,128]{3,2,1,0:T(4,128)(2,1)S(1)}, u32[]{:S(2)}, u32[]{:S(2)}) async-start(bf16[64,1,4,128]{3,2,1,0:T(4,128)(2,1)} %copy.46), calls=%async_computation.1 | async-start | bytes 131072 | tf_op jit(solution)/shard_map/all_to_all | solution.py:51
where the time goes:
time: 123 us; the launch traced here: 122 us
  blocking collectives  35.3 us (29%)
  starting transfers between devices  27.3 us (22%)
  local copies, waits for them, and re-layouts  25.7 us (21%)
  waiting for transfers between devices  18.3 us (15%)
  other arithmetic  10.9 us (9%)
  matrix products  3.56 us (3%)
    all_gather x1, blocking collectives, on_device(): lax.all_gather(hidden, 'rank', axis=3, tiled=True)  19.5 us
    all_gather x1, blocking collectives, on_device(): whole_rows = lax.all_gather(current, 'rank', axis=3, tiled=True)  15.8 us
    all_to_all x1, starting transfers between devices, on_device(): lax.all_to_all(outgoing, 'cache', split_axis=1, concat_axis=0, tiled=True)  14.8 us
    all_to_all x1, starting transfers between devices, finish(): lax.all_to_all(result, 'cache', split_axis=0, concat_axis=1, tiled=True)  12.4 us
    gather x6, local copies, waits for them, and re-layouts, one_turn(): jnp.take(key_cache, chosen, axis=0)  10.2 us
    gather x6, local copies, waits for them, and re-layouts, one_turn(): jnp.take(value_cache, chosen, axis=0)  10.2 us
    all_to_all x1, waiting for transfers between devices, finish(): lax.all_to_all(result, 'cache', split_axis=0, concat_axis=1, tiled=True)  9.87 us
    all_to_all x1, waiting for transfers between devices, on_device(): lax.all_to_all(outgoing, 'cache', split_axis=1, concat_axis=0, tiled=True)  8.45 us
  transfers between devices with their start and end apart: 2, of which 2 were waited for; matrix products, arithmetic and copies ran while one was open for 0% of the time, Pallas kernels for 0%

commit v1 on v0

v1 whole, which is shorter than its diff:
```python
import functools

import jax
import jax.numpy as jnp
from jax import lax
from jax.experimental import pallas as pl
from jax.experimental.pallas import tpu as pltpu
from jax.sharding import PartitionSpec as P

BLOCK = 128
EPSILON = 1e-05
CHUNKS = 2
KEY_TILE = 512
F32 = jnp.float32
BF16 = jnp.bfloat16


def silu(values):
    half = values * 0.5
    return half + half * jnp.tanh(half)


def layer_kernel(
    caches, ranks, cpr,
    cand, listed, hist_len, block_mask, keys, values, w_query, w_gate, w_out,
    ranked,
    cand_v, listed_v, length_s, mask_s, keys_v, values_v, w_in_v, w_out_v, place, send1, gathered, hidden, send2, recv2,
    load_sem, a_send, a_recv, ring_send, ring_recv, b_send, b_recv,
):
    my_cache = lax.axis_index("cache")
    my_rank = lax.axis_index("rank")
    rows = caches * cpr
    part = rows // CHUNKS
    head = keys.shape[1]
    hist = keys.shape[0]
    right = lax.rem(my_rank + 1, ranks)
    left = lax.rem(my_rank + ranks - 1, ranks)

    loads = [
        pltpu.make_async_copy(cand, cand_v, load_sem.at[0]),
        pltpu.make_async_copy(w_query, w_in_v.at[:, pl.ds(0, head)], load_sem.at[1]),
        pltpu.make_async_copy(w_gate, w_in_v.at[:, pl.ds(head, head)], load_sem.at[2]),
        pltpu.make_async_copy(values, values_v, load_sem.at[3]),
        pltpu.make_async_copy(keys, keys_v, load_sem.at[4]),
        pltpu.make_async_copy(w_out, w_out_v, load_sem.at[5]),
        pltpu.make_async_copy(listed, listed_v, load_sem.at[6]),
        pltpu.make_async_copy(hist_len, length_s, load_sem.at[7]),
        pltpu.make_async_copy(block_mask, mask_s, load_sem.at[8]),
    ]
    for load in loads:
        load.start()

    barrier = pltpu.get_barrier_semaphore()

    def greet(step, carry):
        peer = lax.rem(my_cache + step, caches)
        pl.semaphore_signal(barrier, inc=1, device_id={"cache": peer}, device_id_type=pl.DeviceIdType.MESH)
        return carry

    lax.fori_loop(1, caches, greet, 0)
    for peer in (left, right):
        pl.semaphore_signal(barrier, inc=1, device_id={"rank": peer}, device_id_type=pl.DeviceIdType.MESH)

    users = caches
    slot_of = (
        lax.broadcasted_iota(jnp.int32, (users, rows), 1) // cpr
        == lax.broadcasted_iota(jnp.int32, (users, rows), 0)
    ).astype(F32).astype(BF16)
    loads[6].wait()
    listed_rows = jnp.broadcast_to(listed_v[...].astype(F32), (8, users)).astype(BF16)
    user_of = jnp.dot(listed_rows, slot_of, preferred_element_type=F32)[0:1, :]
    column = lax.broadcasted_iota(jnp.int32, (1, rows), 1)
    target = user_of * cpr + lax.rem(column, cpr).astype(F32)
    row_no = lax.broadcasted_iota(jnp.int32, (rows, rows), 0).astype(F32)
    moved = jnp.where(row_no == target, 1.0, 0.0)
    place[...] = moved.T.astype(BF16)
    loads[0].wait()
    send1[...] = jnp.dot(
        moved.astype(BF16), cand_v[...], preferred_element_type=F32
    ).astype(BF16)

    pl.semaphore_wait(barrier, caches - 1 + 2)

    def send_user(step, carry):
        peer = lax.rem(my_cache + step, caches)
        pltpu.make_async_remote_copy(
            src_ref=send1.at[pl.ds(pl.multiple_of(peer * cpr, cpr), cpr)],
            dst_ref=gathered.at[my_rank, pl.ds(pl.multiple_of(my_cache * cpr, cpr), cpr)],
            send_sem=a_send,
            recv_sem=a_recv,
            device_id={"cache": peer},
            device_id_type=pl.DeviceIdType.MESH,
        ).start()
        return carry

    lax.fori_loop(1, caches, send_user, 0)
    mine = pl.ds(pl.multiple_of(my_cache * cpr, cpr), cpr)
    pltpu.make_async_copy(send1.at[mine], gathered.at[my_rank, mine], a_recv).start()

    loads[3].wait()
    loads[7].wait()
    loads[8].wait()
    length = length_s[0]
    for block in range(hist // BLOCK):
        events = pl.ds(block * BLOCK, BLOCK)
        limit = (length - block * BLOCK) * (mask_s[0, block] == 1).astype(jnp.int32)
        live = (lax.broadcasted_iota(jnp.int32, (BLOCK, head), 0) < limit).astype(F32)
        values_v[events, :] = (values_v[events, :].astype(F32) * live).astype(BF16)

    for load in (loads[1], loads[2], loads[4], loads[5]):
        load.wait()
    pltpu.make_async_copy(gathered.at[my_rank], gathered.at[my_rank], a_recv).wait()

    def ring_copy(buffer, phase, chunk, way, step):
        owner = lax.rem(my_rank + (ranks - step if way == 0 else step), ranks)
        span = pl.ds(chunk * part, part)
        return pltpu.make_async_remote_copy(
            src_ref=buffer.at[owner, span],
            dst_ref=buffer.at[owner, span],
            send_sem=ring_send.at[phase, chunk, way, step],
            recv_sem=ring_recv.at[phase, chunk, way, step],
            device_id={"rank": right if way == 0 else left},
            device_id_type=pl.DeviceIdType.MESH,
        )

    half = ranks // 2

    def steps_of(chunk, way):
        return half if (chunk % 2 == 0) == (way == 0) else half - 1

    def ring_wait(buffer, phase, chunk, way, step):
        ring_copy(buffer, phase, chunk, way, step).wait_recv()

    def ring_forward(buffer, phase, chunk, step):
        for way in (0, 1):
            if step > 0 and step - 1 < steps_of(chunk, way):
                ring_wait(buffer, phase, chunk, way, step - 1)
            if step < steps_of(chunk, way):
                ring_copy(buffer, phase, chunk, way, step).start()

    for step in range(half):
        for chunk in range(CHUNKS):
            ring_forward(gathered, 0, chunk, step)

    for chunk in range(CHUNKS):
        ring_forward(gathered, 0, chunk, half)
        span = pl.ds(chunk * part, part)
        slices = [gathered[k, span, :].astype(F32) for k in range(ranks)]
        centre = jnp.sum(sum(slices[1:], slices[0]), axis=-1, keepdims=True) * (1.0 / (ranks * head))
        slices = [s - centre for s in slices]
        squares = [s * s for s in slices]
        spread = jnp.sum(sum(squares[1:], squares[0]), axis=-1, keepdims=True) * (1.0 / (ranks * head))
        factor = lax.rsqrt(spread + EPSILON)
        normed = jnp.concatenate([(s * factor).astype(BF16) for s in slices], axis=1)
        both = silu(jnp.dot(normed, w_in_v[...], preferred_element_type=F32))
        queries = both[:, :head].astype(BF16)
        gate = both[:, head:]
        attended = jnp.zeros((part, head), F32)
        for tile in range(hist // KEY_TILE):
            events = pl.ds(tile * KEY_TILE, KEY_TILE)
            scores = lax.dot_general(
                queries, keys_v[events, :], (((1,), (1,)), ((), ())), preferred_element_type=F32
            )
            weights = silu(scores * (head ** -0.5)).astype(BF16)
            attended += jnp.dot(weights, values_v[events, :], preferred_element_type=F32)
        centre = jnp.mean(attended, axis=-1, keepdims=True)
        attended = attended - centre
        spread = jnp.mean(attended * attended, axis=-1, keepdims=True)
        hidden[my_rank, span, :] = (attended * lax.rsqrt(spread + EPSILON) * gate).astype(BF16)
        ring_forward(hidden, 1, chunk, 0)

    for step in range(1, half):
        for chunk in range(CHUNKS):
            ring_forward(hidden, 1, chunk, step)

    shards = caches // CHUNKS
    for chunk in range(CHUNKS):
        ring_forward(hidden, 1, chunk, half)
        span = pl.ds(chunk * part, part)
        whole = jnp.concatenate([hidden[k, span, :] for k in range(ranks)], axis=1)
        projected = jnp.dot(whole, w_out_v[...], preferred_element_type=F32)
        send2[span, :] = (gathered[my_rank, span, :].astype(F32) + projected).astype(BF16)

        def send_shard(step, carry, chunk=chunk):
            peer = chunk * shards + lax.rem(my_cache + step, shards)
            there = pl.ds(pl.multiple_of(peer * cpr, cpr), cpr)

            @pl.when(peer != my_cache)
            def _():
                pltpu.make_async_remote_copy(
                    src_ref=send2.at[there],
                    dst_ref=recv2.at[mine],
                    send_sem=b_send,
                    recv_sem=b_recv,
                    device_id={"cache": peer},
                    device_id_type=pl.DeviceIdType.MESH,
                ).start()

            @pl.when(peer == my_cache)
            def _():
                pltpu.make_async_copy(send2.at[mine], recv2.at[mine], b_recv).start()

            return carry

        lax.fori_loop(0, shards, send_shard, 0)

    pltpu.make_async_copy(recv2, recv2, b_recv).wait()
    ranked[...] = jnp.dot(place[...], recv2[...], preferred_element_type=F32).astype(BF16)

    others = pl.ds(0, rows - cpr)
    pltpu.make_async_copy(send1.at[others], send1.at[others], a_send).wait()
    pltpu.make_async_copy(send2.at[others], send2.at[others], b_send).wait()
    for phase, buffer in ((0, gathered), (1, hidden)):
        for chunk in range(CHUNKS):
            for way in (0, 1):
                for step in range(steps_of(chunk, way)):
                    ring_copy(buffer, phase, chunk, way, step).wait_send()


def on_device(
    cand_rows, listed, hist_len, block_mask, hist_keys, hist_values, w_query, w_gate, w_out, *, caches, ranks
):
    _, users, cpr, width = cand_rows.shape
    rows = users * cpr
    hist = hist_keys.shape[2]
    depth = w_query.shape[1]
    in_hbm = pl.BlockSpec(memory_space=pltpu.HBM)
    vmem = pl.BlockSpec(memory_space=pltpu.VMEM)
    half = ranks // 2
    ranked = pl.pallas_call(
        functools.partial(layer_kernel, caches, ranks, cpr),
        out_shape=jax.ShapeDtypeStruct((rows, width), BF16),
        in_specs=[in_hbm] * 9,
        out_specs=vmem,
        scratch_shapes=[
            pltpu.VMEM((rows, width), BF16),
            pltpu.VMEM((1, users), jnp.int32),
            pltpu.SMEM(hist_len.shape, jnp.int32),
            pltpu.SMEM(block_mask.shape, jnp.int32),
            pltpu.VMEM((hist, width), BF16),
            pltpu.VMEM((hist, width), BF16),
            pltpu.VMEM((depth, 2 * width), BF16),
            pltpu.VMEM((depth, width), BF16),
            pltpu.VMEM((rows, rows), BF16),
            pltpu.VMEM((rows, width), BF16),
            pltpu.VMEM((ranks, rows, width), BF16),
            pltpu.VMEM((ranks, rows, width), BF16),
            pltpu.VMEM((rows, width), BF16),
            pltpu.VMEM((rows, width), BF16),
            pltpu.SemaphoreType.DMA((9,)),
            pltpu.SemaphoreType.DMA,
            pltpu.SemaphoreType.DMA,
            pltpu.SemaphoreType.DMA((2, CHUNKS, 2, half)),
            pltpu.SemaphoreType.DMA((2, CHUNKS, 2, half)),
            pltpu.SemaphoreType.DMA,
            pltpu.SemaphoreType.DMA,
        ],
        compiler_params=pltpu.CompilerParams(
            collective_id=0, has_side_effects=True, vmem_limit_bytes=56 * 1024 * 1024
        ),
        name="hstu_layer",
    )(
        cand_rows.reshape(rows, width),
        listed.reshape(1, users),
        hist_len,
        block_mask,
        hist_keys.reshape(hist, width),
        hist_values.reshape(hist, width),
        w_query.reshape(depth, width),
        w_gate.reshape(depth, width),
        w_out.reshape(depth, width),
    )
    return ranked.reshape(cand_rows.shape)


def solution(mesh):
    placed = (
        P("cache", None, None, "rank"),
        P(),
        P("cache"),
        P("cache", None),
        P(None, "cache", None, "rank"),
        P(None, "cache", None, "rank"),
        P(None, None, "rank"),
        P(None, None, "rank"),
        P(None, None, "rank"),
    )
    return jax.shard_map(
        functools.partial(on_device, caches=mesh.shape["cache"], ranks=mesh.shape["rank"]),
        mesh=mesh,
        in_specs=placed,
        out_specs=P("cache", None, None, "rank"),
        check_vma=False,
    )
```

time: 123 us -> 59.5 us (0.48)
  Pallas kernels: 0 us -> 57.1 us
  blocking collectives: 35.3 us -> 0 us
  starting transfers between devices: 27.3 us -> 0 us
  local copies, waits for them, and re-layouts: 25.7 us -> 1.49 us
  waiting for transfers between devices: 18.3 us -> 0 us
  other arithmetic: 10.9 us -> 0 us
  matrix products: 3.56 us -> 0 us
    pallas_call x0 -> x1, Pallas kernels: none -> 57.1 us  [on_device(): pl.pallas_call(functools.partial(layer_kernel, caches, ranks, cpr), out_s...]
    all_gather x2 -> x0, blocking collectives: 35.3 us -> none  [the longest x1 19.5 us: on_device(): lax.all_gather(hidden, 'rank', axis=3, tiled=True)]
    all_to_all x2 -> x0, starting transfers between devices: 27.3 us -> none  [the longest x1 14.8 us: on_device(): lax.all_to_all(outgoing, 'cache', split_axis=1, concat_axis=0, tiled=True)]
    gather x14 -> x0, local copies, waits for them, and re-layouts: 22.6 us -> none  [the longest x6 10.2 us: one_turn(): jnp.take(key_cache, chosen, axis=0)]
    all_to_all x2 -> x0, waiting for transfers between devices: 18.3 us -> none  [the longest x1 9.87 us: finish(): lax.all_to_all(result, 'cache', split_axis=0, concat_axis=1, tiled=True)]
    convert_element_type x6 -> x0, other arithmetic: 4.3 us -> none  [one_turn(): ((places < length) & jnp.repeat(chosen_live, BLOCK)).astype(jnp.float32)]
    dot_general x9 -> x0, matrix products: 3.56 us -> none  [the longest x6 2.63 us: one_turn(): jnp.einsum('nkht,the->nkhe', weights, value_rows, preferred_element_type=...]
    select_n x10 -> x0, other arithmetic: 2.11 us -> none  [the longest x2 0.77 us: on_device(): outgoing = jnp.take(cand_rows, slot_of_user, axis=1)]
  transfers between devices with their start and end apart: 2 -> 0, of which waited for: 2 -> 0; matrix products, arithmetic and copies ran while one was open for 0% -> 0% of each run, Pallas kernels for 0% -> 0%
where the time goes in v1:
time: 59.5 us; the launch traced here: 59.3 us
  Pallas kernels  57.1 us (96%)
  local copies, waits for them, and re-layouts  1.49 us (3%)
  between operations  0.66 us (1%)
    pallas_call x1, Pallas kernels, on_device(): pl.pallas_call(functools.partial(layer_kernel, caches, ranks, cpr), out_s...  57.1 us
    unnamed x1, local copies, waits for them, and re-layouts  1.49 us

profile of v1, /device:TPU:1, one launch (start us, length us, event | category | flops | bytes accessed | tf_op | source)
XLA Modules:
  0.0 59.3 jit_solution(162180794750081498)
XLA Ops:
  0.7 57.1 %hstu_layer.1 = bf16[256,128]{1,0:T(8,128)(2,1)} custom-call(bf16[256,128]{1,0:T(8,128)(2,1)} %bitcast.14, s32[1,64]{1,0:T(1,128)} %bitcast.15, s32[1]{0:T(128)S(6)} %copy.11.hist_len, s32[1,24]{1,0:T(1,128)} %block_mask.1, bf16[3072,128]{1,0:T(8,128)(2,1)} %bitcast.8, bf16[3072,128]{1,0:T(8,128)(2,1)} %bitcast.9, bf16[1024,128]{1,0:T(8,128)(2,1)} %bitcast.10, ...), custom_call_target="tpu_custom_call" | custom-call | tf_op jit(solution)/shard_map/hstu_layer/pallas_call | solution.py:230
  57.8 1.5 %copy.12 = bf16[1,64,4,128]{3,2,1,0:T(4,128)(2,1)} copy(bf16[1,64,4,128]{3,2,1,0:T(4,128)(2,1)} %bitcast.13) | data formatting | bytes 131072

commit v2 on v1

v2 whole, which is shorter than its diff:
```python
import functools

import jax
import jax.numpy as jnp
from jax import lax
from jax.experimental import pallas as pl
from jax.experimental.pallas import tpu as pltpu
from jax.sharding import PartitionSpec as P

BLOCK = 128
EPSILON = 1e-05
CHUNKS = 2
KEY_TILE = 512
F32 = jnp.float32
BF16 = jnp.bfloat16


def silu(values):
    half = values * 0.5
    return half + half * jnp.tanh(half)


DEPTHS = 8
MESH = pl.DeviceIdType.MESH
FAR_X = (2, 1, 3, 0)


def layer_kernel(
    caches, ranks, cpr,
    cand, listed, hist_len, block_mask, keys, values, w_query, w_gate, w_out,
    ranked,
    cand_v, listed_v, length_s, mask_s, keys_v, values_v, w_in_v, w_out_v, place, send1, gathered, hidden,
    send2, recv2, load_sem, a_send, a_recv, near_recv, rest_recv, ring_send, b_send, b_recv,
):
    my_cache = lax.axis_index("cache")
    my_rank = lax.axis_index("rank")
    rows = caches * cpr
    part = rows // CHUNKS
    head = keys.shape[1]
    hist = keys.shape[0]
    wide = caches // (2 * DEPTHS)
    my_core = lax.rem(my_cache, 2)
    my_z = lax.rem(my_cache // 2, DEPTHS)
    my_x = my_cache // (2 * DEPTHS)

    barrier = pltpu.get_barrier_semaphore()

    def peer_at(dx, dz, dc):
        x, z, core = lax.rem(my_x + dx, wide), lax.rem(my_z + dz, DEPTHS), lax.rem(my_core + dc, 2)
        return (x * DEPTHS + z) * 2 + core

    def back(step, extent):
        return (extent - step) % extent if isinstance(step, int) else lax.rem(extent - step, extent)

    def for_depths(places, body):
        def one(step, carry):
            away = (step + 1) // 2
            dz = lax.rem(DEPTHS + DEPTHS // 2 + away * (1 - 2 * lax.rem(step, 2)), DEPTHS)
            for dx in places:
                for dc in (0, 1):
                    body(dx, dz, dc)
            return carry

        lax.fori_loop(0, DEPTHS - 1, one, 0)
        for dx in places:
            for dc in (0, 1):
                if (dx, dc) != (0, 0):
                    body(dx, 0, dc)

    def greet(dx, dz, dc):
        pl.semaphore_signal(
            barrier, inc=1, device_id={"cache": peer_at(dx, dz, dc)}, device_id_type=MESH
        )

    for_depths(FAR_X, greet)

    def rank_at(step):
        return lax.rem(my_rank + (step + ranks), ranks)

    for step in (-2, -1, 1, 2):
        pl.semaphore_signal(barrier, inc=1, device_id={"rank": rank_at(step)}, device_id_type=MESH)

    def load(source, target, number):
        return pltpu.make_async_copy(source, target, load_sem.at[number])

    loads = [
        load(cand, cand_v, 0),
        load(listed, listed_v, 1),
        load(values, values_v, 2),
        load(hist_len, length_s, 3),
        load(block_mask, mask_s, 4),
        load(keys, keys_v, 5),
        load(w_query, w_in_v.at[:, pl.ds(0, head)], 6),
        load(w_gate, w_in_v.at[:, pl.ds(head, head)], 7),
        load(w_out, w_out_v, 8),
    ]
    for one in loads:
        one.start()

    users = caches
    slot_of = (
        lax.broadcasted_iota(jnp.int32, (users, rows), 1) // cpr
        == lax.broadcasted_iota(jnp.int32, (users, rows), 0)
    ).astype(F32).astype(BF16)
    loads[1].wait()
    listed_rows = jnp.broadcast_to(listed_v[...].astype(F32), (8, users)).astype(BF16)
    user_of = jnp.dot(listed_rows, slot_of, preferred_element_type=F32)[0:1, :]
    column = lax.broadcasted_iota(jnp.int32, (1, rows), 1)
    target = user_of * cpr + lax.rem(column, cpr).astype(F32)
    row_no = lax.broadcasted_iota(jnp.int32, (rows, rows), 0).astype(F32)
    moved = jnp.where(row_no == target, 1.0, 0.0)
    loads[0].wait()
    send1[...] = jnp.dot(
        moved.astype(BF16), cand_v[...], preferred_element_type=F32
    ).astype(BF16)

    pl.semaphore_wait(barrier, caches - 1 + 4)

    def of_user(user):
        return pl.ds(pl.multiple_of(user * cpr, cpr), cpr)

    def of_place(dx, dz, dc):
        return pl.ds(pl.multiple_of(((FAR_X.index(dx) * DEPTHS + dz) * 2 + dc) * cpr, cpr), cpr)

    def send_user(dx, dz, dc):
        peer = peer_at(dx, dz, dc)
        pltpu.make_async_remote_copy(
            src_ref=send1.at[of_user(peer)],
            dst_ref=gathered.at[my_rank, of_place(back(dx, wide), back(dz, DEPTHS), dc)],
            send_sem=a_send,
            recv_sem=a_recv,
            device_id={"cache": peer},
            device_id_type=MESH,
        ).start()

    for_depths(FAR_X, send_user)
    mine, here = of_user(my_cache), of_place(0, 0, 0)
    pltpu.make_async_copy(send1.at[mine], gathered.at[my_rank, here], a_recv).start()

    place[...] = moved.T.astype(BF16)
    for number in (2, 3, 4):
        loads[number].wait()
    length = length_s[0]
    for block in range(hist // BLOCK):
        events = pl.ds(block * BLOCK, BLOCK)
        limit = (length - block * BLOCK) * (mask_s[0, block] == 1).astype(jnp.int32)
        live = (lax.broadcasted_iota(jnp.int32, (BLOCK, head), 0) < limit).astype(F32)
        values_v[events, :] = (values_v[events, :].astype(F32) * live).astype(BF16)
    for number in (5, 6, 7, 8):
        loads[number].wait()
    pltpu.make_async_copy(gathered.at[my_rank], gathered.at[my_rank], a_recv).wait()

    def hop(buffer, phase, chunk, slot, step, recv_sem):
        block = buffer.at[rank_at(slot), pl.ds(chunk * part, part)]
        return pltpu.make_async_remote_copy(
            src_ref=block,
            dst_ref=block,
            send_sem=ring_send.at[phase],
            recv_sem=recv_sem,
            device_id={"rank": rank_at(step)},
            device_id_type=MESH,
        )

    def spread(buffer, phase, chunk):
        for way, step in ((0, 2), (1, -2)):
            hop(buffer, phase, chunk, 0, step, near_recv.at[phase, chunk, way]).start()
        for step in (1, -1):
            hop(buffer, phase, chunk, 0, step, rest_recv.at[phase, chunk]).start()

    def relay(buffer, phase, chunk):
        for way, step in ((0, 1), (1, -1)):
            hop(buffer, phase, chunk, -2 * step, 2 * step, near_recv.at[phase, chunk, way]).wait_recv()
            hop(buffer, phase, chunk, -2 * step, step, rest_recv.at[phase, chunk]).start()
            if chunk % 2 == way:
                hop(buffer, phase, chunk, -2 * step, 2 * step, rest_recv.at[phase, chunk]).start()

    def complete(buffer, phase, chunk):
        five = buffer.at[pl.ds(0, 5), pl.ds(chunk * part, part)]
        pltpu.make_async_copy(five, five, rest_recv.at[phase, chunk]).wait()

    for chunk in range(CHUNKS):
        spread(gathered, 0, chunk)
    for chunk in range(CHUNKS):
        relay(gathered, 0, chunk)

    for chunk in range(CHUNKS):
        complete(gathered, 0, chunk)
        span = pl.ds(chunk * part, part)
        slices = [gathered[k, span, :].astype(F32) for k in range(ranks)]
        centre = jnp.sum(sum(slices[1:], slices[0]), axis=-1, keepdims=True) * (1.0 / (ranks * head))
        slices = [s - centre for s in slices]
        squares = [s * s for s in slices]
        spread_of = jnp.sum(sum(squares[1:], squares[0]), axis=-1, keepdims=True) * (1.0 / (ranks * head))
        factor = lax.rsqrt(spread_of + EPSILON)
        normed = jnp.concatenate([(s * factor).astype(BF16) for s in slices], axis=1)
        both = silu(jnp.dot(normed, w_in_v[...], preferred_element_type=F32))
        queries = both[:, :head].astype(BF16)
        gate = both[:, head:]
        attended = jnp.zeros((part, head), F32)
        for tile in range(hist // KEY_TILE):
            events = pl.ds(tile * KEY_TILE, KEY_TILE)
            scores = lax.dot_general(
                queries, keys_v[events, :], (((1,), (1,)), ((), ())), preferred_element_type=F32
            )
            weights = silu(scores * (head ** -0.5)).astype(BF16)
            attended += jnp.dot(weights, values_v[events, :], preferred_element_type=F32)
        centre = jnp.mean(attended, axis=-1, keepdims=True)
        attended = attended - centre
        spread_of = jnp.mean(attended * attended, axis=-1, keepdims=True)
        hidden[my_rank, span, :] = (attended * lax.rsqrt(spread_of + EPSILON) * gate).astype(BF16)
        spread(hidden, 1, chunk)

    for chunk in range(CHUNKS):
        relay(hidden, 1, chunk)

    for chunk in range(CHUNKS):
        complete(hidden, 1, chunk)
        span = pl.ds(chunk * part, part)
        whole = jnp.concatenate([hidden[k, span, :] for k in range(ranks)], axis=1)
        projected = jnp.dot(whole, w_out_v[...], preferred_element_type=F32)
        send2[span, :] = (gathered[my_rank, span, :].astype(F32) + projected).astype(BF16)

        def send_shard(dx, dz, dc):
            pltpu.make_async_remote_copy(
                src_ref=send2.at[of_place(dx, dz, dc)],
                dst_ref=recv2.at[mine],
                send_sem=b_send,
                recv_sem=b_recv,
                device_id={"cache": peer_at(dx, dz, dc)},
                device_id_type=MESH,
            ).start()

        count = wide // CHUNKS
        for_depths(FAR_X[chunk * count:(chunk + 1) * count], send_shard)
    pltpu.make_async_copy(send2.at[here], recv2.at[mine], b_recv).start()

    pltpu.make_async_copy(recv2, recv2, b_recv).wait()
    ranked[...] = jnp.dot(place[...], recv2[...], preferred_element_type=F32).astype(BF16)

    others = pl.ds(0, rows - cpr)
    pltpu.make_async_copy(send1.at[others], send1.at[others], a_send).wait()
    pltpu.make_async_copy(send2.at[others], send2.at[others], b_send).wait()
    for phase, buffer in ((0, gathered), (1, hidden)):
        seven = buffer.at[pl.ds(0, ranks - 1)]
        pltpu.make_async_copy(seven, seven, ring_send.at[phase]).wait()


def on_device(
    cand_rows, listed, hist_len, block_mask, hist_keys, hist_values, w_query, w_gate, w_out, *, caches, ranks
):
    _, users, cpr, width = cand_rows.shape
    rows = users * cpr
    hist = hist_keys.shape[2]
    depth = w_query.shape[1]
    in_hbm = pl.BlockSpec(memory_space=pltpu.HBM)
    vmem = pl.BlockSpec(memory_space=pltpu.VMEM)
    ranked = pl.pallas_call(
        functools.partial(layer_kernel, caches, ranks, cpr),
        out_shape=jax.ShapeDtypeStruct((rows, width), BF16),
        in_specs=[in_hbm] * 9,
        out_specs=vmem,
        scratch_shapes=[
            pltpu.VMEM((rows, width), BF16),
            pltpu.VMEM((1, users), jnp.int32),
            pltpu.SMEM(hist_len.shape, jnp.int32),
            pltpu.SMEM(block_mask.shape, jnp.int32),
            pltpu.VMEM((hist, width), BF16),
            pltpu.VMEM((hist, width), BF16),
            pltpu.VMEM((depth, 2 * width), BF16),
            pltpu.VMEM((depth, width), BF16),
            pltpu.VMEM((rows, rows), BF16),
            pltpu.VMEM((rows, width), BF16),
            pltpu.VMEM((ranks, rows, width), BF16),
            pltpu.VMEM((ranks, rows, width), BF16),
            pltpu.VMEM((rows, width), BF16),
            pltpu.VMEM((rows, width), BF16),
            pltpu.SemaphoreType.DMA((9,)),
            pltpu.SemaphoreType.DMA,
            pltpu.SemaphoreType.DMA,
            pltpu.SemaphoreType.DMA((2, CHUNKS, 2)),
            pltpu.SemaphoreType.DMA((2, CHUNKS)),
            pltpu.SemaphoreType.DMA((2,)),
            pltpu.SemaphoreType.DMA,
            pltpu.SemaphoreType.DMA,
        ],
        compiler_params=pltpu.CompilerParams(
            collective_id=0, has_side_effects=True, vmem_limit_bytes=(53 * 1024 + 850) * 1024
        ),
        name="hstu_layer",
    )(
        cand_rows.reshape(rows, width),
        listed.reshape(1, users),
        hist_len,
        block_mask,
        hist_keys.reshape(hist, width),
        hist_values.reshape(hist, width),
        w_query.reshape(depth, width),
        w_gate.reshape(depth, width),
        w_out.reshape(depth, width),
    )
    return ranked.reshape(cand_rows.shape)


def solution(mesh):
    placed = (
        P("cache", None, None, "rank"),
        P(),
        P("cache"),
        P("cache", None),
        P(None, "cache", None, "rank"),
        P(None, "cache", None, "rank"),
        P(None, None, "rank"),
        P(None, None, "rank"),
        P(None, None, "rank"),
    )
    return jax.shard_map(
        functools.partial(on_device, caches=mesh.shape["cache"], ranks=mesh.shape["rank"]),
        mesh=mesh,
        in_specs=placed,
        out_specs=P("cache", None, None, "rank"),
        check_vma=False,
    )
```

time: 59.5 us -> 51.1 us (0.86)
  Pallas kernels: 57.1 us -> 49 us
    pallas_call x1, Pallas kernels: 57.1 us -> 49 us  [on_device(): pl.pallas_call(functools.partial(layer_kernel, caches, ranks, cpr), out_s...]
    unnamed x1 -> x5, local copies, waits for them, and re-layouts: 1.49 us -> 1.29 us
where the time goes in v2:
time: 51.1 us; the launch traced here: 51 us
  Pallas kernels  49 us (96%)
  local copies, waits for them, and re-layouts  1.29 us (3%)
  between operations  0.68 us (1%)
    pallas_call x1, Pallas kernels, on_device(): pl.pallas_call(functools.partial(layer_kernel, caches, ranks, cpr), out_s...  49 us
    unnamed x5, local copies, waits for them, and re-layouts  1.29 us

profile of v2, /device:TPU:1, one launch (start us, length us, event | category | flops | bytes accessed | tf_op | source)
XLA Modules:
  0.0 51.0 jit_solution(9058965202561584813)
XLA Ops:
  0.7 0.0 copy-start
  0.7 0.0 copy-start.1
  0.7 0.6 %copy-done = s32[64]{0:T(128)S(1)} copy-done((s32[64]{0:T(128)S(1)}, s32[64]{0:T(128)}, u32[]{:S(2)}) %copy-start) | copy-done | bytes 280
  1.3 0.0 copy-done.1
  1.3 49.0 %hstu_layer.1 = bf16[256,128]{1,0:T(8,128)(2,1)S(1)} custom-call(bf16[256,128]{1,0:T(8,128)(2,1)} %bitcast.15, s32[1,64]{1,0:T(1,128)S(1)} %bitcast.9, s32[1]{0:T(128)S(6)} %copy.11.hist_len, s32[1,24]{1,0:T(1,128)S(1)} %copy-done.1, bf16[3072,128]{1,0:T(8,128)(2,1)} %bitcast.10, bf16[3072,128]{1,0:T(8,128)(2,1)} %bitcast.11, bf16[1024,128]{1,0:T(8,128)(2,1)} %bitcast.12, ...), custom_call_target="tpu_custom_call" | custom-call | tf_op jit(solution)/shard_map/hstu_layer/pallas_call | solution.py:257
  50.3 0.6 %copy.12 = bf16[1,64,4,128]{3,2,1,0:T(4,128)(2,1)} copy(bf16[1,64,4,128]{3,2,1,0:T(4,128)(2,1)S(1)} %bitcast.8) | data formatting | bytes 131072
Async XLA Ops:
  0.7 0.7 %copy-start = (s32[64]{0:T(128)S(1)}, s32[64]{0:T(128)}, u32[]{:S(2)}) copy-start(s32[64]{0:T(128)} %param.10) | copy-start | bytes 772
  0.7 0.7 %copy-start.1 = (s32[1,24]{1,0:T(1,128)S(1)}, s32[1,24]{1,0:T(1,128)}, u32[]{:S(2)}) copy-start(s32[1,24]{1,0:T(1,128)} %block_mask.1) | copy-start | bytes 292

commit v3 on v2

--- a/solution.py
+++ b/solution.py
@@ -10,13 +10,13 @@
 BLOCK = 128
 EPSILON = 1e-05
 CHUNKS = 2
-KEY_TILE = 512
+PIECES = 4
+KEY_TILE = 1024
 F32 = jnp.float32
 BF16 = jnp.bfloat16
 
 
-def silu(values):
-    half = values * 0.5
+def silu_of_twice(half):
     return half + half * jnp.tanh(half)
 
 
@@ -27,9 +27,9 @@
 
 def layer_kernel(
     caches, ranks, cpr,
-    cand, listed, hist_len, block_mask, keys, values, w_query, w_gate, w_out,
+    cand, listed, block_mask, keys, values, w_query, w_gate, w_out, hist_len,
     ranked,
-    cand_v, listed_v, length_s, mask_s, keys_v, values_v, w_in_v, w_out_v, place, send1, gathered, hidden,
+    cand_v, listed_v, mask_s, keys_v, values_v, w_in_v, w_out_v, place, send1, gathered, hidden,
     send2, recv2, load_sem, a_send, a_recv, near_recv, rest_recv, ring_send, b_send, b_recv,
 ):
     my_cache = lax.axis_index("cache")
@@ -87,12 +87,11 @@
         load(cand, cand_v, 0),
         load(listed, listed_v, 1),
         load(values, values_v, 2),
-        load(hist_len, length_s, 3),
-        load(block_mask, mask_s, 4),
-        load(keys, keys_v, 5),
-        load(w_query, w_in_v.at[:, pl.ds(0, head)], 6),
-        load(w_gate, w_in_v.at[:, pl.ds(head, head)], 7),
-        load(w_out, w_out_v, 8),
+        load(block_mask, mask_s, 3),
+        load(keys, keys_v, 4),
+        load(w_query, w_in_v.at[:, pl.ds(0, head)], 5),
+        load(w_gate, w_in_v.at[:, pl.ds(head, head)], 6),
+        load(w_out, w_out_v, 7),
     ]
     for one in loads:
         one.start()
@@ -138,20 +137,23 @@
     pltpu.make_async_copy(send1.at[mine], gathered.at[my_rank, here], a_recv).start()
 
     place[...] = moved.T.astype(BF16)
-    for number in (2, 3, 4):
+    for number in (2, 3):
         loads[number].wait()
-    length = length_s[0]
+    length = hist_len[0]
     for block in range(hist // BLOCK):
         events = pl.ds(block * BLOCK, BLOCK)
         limit = (length - block * BLOCK) * (mask_s[0, block] == 1).astype(jnp.int32)
         live = (lax.broadcasted_iota(jnp.int32, (BLOCK, head), 0) < limit).astype(F32)
         values_v[events, :] = (values_v[events, :].astype(F32) * live).astype(BF16)
-    for number in (5, 6, 7, 8):
+    for number in (4, 5, 6, 7):
         loads[number].wait()
     pltpu.make_async_copy(gathered.at[my_rank], gathered.at[my_rank], a_recv).wait()
 
-    def hop(buffer, phase, chunk, slot, step, recv_sem):
-        block = buffer.at[rank_at(slot), pl.ds(chunk * part, part)]
+    small = rows // PIECES
+    of_chunk = [range(c * PIECES // CHUNKS, (c + 1) * PIECES // CHUNKS) for c in range(CHUNKS)]
+
+    def hop(buffer, phase, piece, slot, step, recv_sem):
+        block = buffer.at[rank_at(slot), pl.ds(piece * small, small)]
         return pltpu.make_async_remote_copy(
             src_ref=block,
             dst_ref=block,
@@ -161,25 +163,32 @@
             device_id_type=MESH,
         )
 
-    def spread(buffer, phase, chunk):
-        for way, step in ((0, 2), (1, -2)):
-            hop(buffer, phase, chunk, 0, step, near_recv.at[phase, chunk, way]).start()
-        for step in (1, -1):
-            hop(buffer, phase, chunk, 0, step, rest_recv.at[phase, chunk]).start()
+    def spread_near(buffer, phase, chunk):
+        for piece in of_chunk[chunk]:
+            for way, step in ((0, 2), (1, -2)):
+                hop(buffer, phase, piece, 0, step, near_recv.at[phase, piece, way]).start()
+
+    def spread_next(buffer, phase, chunk):
+        for piece in of_chunk[chunk]:
+            for step in (1, -1):
+                hop(buffer, phase, piece, 0, step, rest_recv.at[phase, chunk]).start()
 
     def relay(buffer, phase, chunk):
-        for way, step in ((0, 1), (1, -1)):
-            hop(buffer, phase, chunk, -2 * step, 2 * step, near_recv.at[phase, chunk, way]).wait_recv()
-            hop(buffer, phase, chunk, -2 * step, step, rest_recv.at[phase, chunk]).start()
-            if chunk % 2 == way:
-                hop(buffer, phase, chunk, -2 * step, 2 * step, rest_recv.at[phase, chunk]).start()
+        for piece in of_chunk[chunk]:
+            for way, step in ((0, 1), (1, -1)):
+                hop(buffer, phase, piece, -2 * step, 2 * step, near_recv.at[phase, piece, way]).wait_recv()
+                hop(buffer, phase, piece, -2 * step, step, rest_recv.at[phase, chunk]).start()
+                if piece % 2 == way:
+                    hop(buffer, phase, piece, -2 * step, 2 * step, rest_recv.at[phase, chunk]).start()
 
     def complete(buffer, phase, chunk):
         five = buffer.at[pl.ds(0, 5), pl.ds(chunk * part, part)]
         pltpu.make_async_copy(five, five, rest_recv.at[phase, chunk]).wait()
 
     for chunk in range(CHUNKS):
-        spread(gathered, 0, chunk)
+        spread_near(gathered, 0, chunk)
+    for chunk in range(CHUNKS):
+        spread_next(gathered, 0, chunk)
     for chunk in range(CHUNKS):
         relay(gathered, 0, chunk)
 
@@ -193,7 +202,7 @@
         spread_of = jnp.sum(sum(squares[1:], squares[0]), axis=-1, keepdims=True) * (1.0 / (ranks * head))
         factor = lax.rsqrt(spread_of + EPSILON)
         normed = jnp.concatenate([(s * factor).astype(BF16) for s in slices], axis=1)
-        both = silu(jnp.dot(normed, w_in_v[...], preferred_element_type=F32))
+        both = silu_of_twice(0.5 * jnp.dot(normed, w_in_v[...], preferred_element_type=F32))
         queries = both[:, :head].astype(BF16)
         gate = both[:, head:]
         attended = jnp.zeros((part, head), F32)
@@ -202,13 +211,14 @@
             scores = lax.dot_general(
                 queries, keys_v[events, :], (((1,), (1,)), ((), ())), preferred_element_type=F32
             )
-            weights = silu(scores * (head ** -0.5)).astype(BF16)
+            weights = silu_of_twice(scores * (0.5 * head ** -0.5)).astype(BF16)
             attended += jnp.dot(weights, values_v[events, :], preferred_element_type=F32)
         centre = jnp.mean(attended, axis=-1, keepdims=True)
         attended = attended - centre
         spread_of = jnp.mean(attended * attended, axis=-1, keepdims=True)
         hidden[my_rank, span, :] = (attended * lax.rsqrt(spread_of + EPSILON) * gate).astype(BF16)
-        spread(hidden, 1, chunk)
+        spread_near(hidden, 1, chunk)
+        spread_next(hidden, 1, chunk)
 
     for chunk in range(CHUNKS):
         relay(hidden, 1, chunk)
@@ -257,12 +267,11 @@
     ranked = pl.pallas_call(
         functools.partial(layer_kernel, caches, ranks, cpr),
         out_shape=jax.ShapeDtypeStruct((rows, width), BF16),
-        in_specs=[in_hbm] * 9,
+        in_specs=[in_hbm] * 8 + [pl.BlockSpec(memory_space=pltpu.SMEM)],
         out_specs=vmem,
         scratch_shapes=[
             pltpu.VMEM((rows, width), BF16),
             pltpu.VMEM((1, users), jnp.int32),
-            pltpu.SMEM(hist_len.shape, jnp.int32),
             pltpu.SMEM(block_mask.shape, jnp.int32),
             pltpu.VMEM((hist, width), BF16),
             pltpu.VMEM((hist, width), BF16),
@@ -274,29 +283,34 @@
             pltpu.VMEM((ranks, rows, width), BF16),
             pltpu.VMEM((rows, width), BF16),
             pltpu.VMEM((rows, width), BF16),
-            pltpu.SemaphoreType.DMA((9,)),
+            pltpu.SemaphoreType.DMA((8,)),
             pltpu.SemaphoreType.DMA,
             pltpu.SemaphoreType.DMA,
-            pltpu.SemaphoreType.DMA((2, CHUNKS, 2)),
+            pltpu.SemaphoreType.DMA((2, PIECES, 2)),
             pltpu.SemaphoreType.DMA((2, CHUNKS)),
             pltpu.SemaphoreType.DMA((2,)),
             pltpu.SemaphoreType.DMA,
             pltpu.SemaphoreType.DMA,
         ],
         compiler_params=pltpu.CompilerParams(
-            collective_id=0, has_side_effects=True, vmem_limit_bytes=(53 * 1024 + 850) * 1024
+            collective_id=0, has_side_effects=True, vmem_limit_bytes=40 * 1024 * 1024
         ),
         name="hstu_layer",
     )(
-        cand_rows.reshape(rows, width),
-        listed.reshape(1, users),
+        *(
+            pltpu.with_memory_space_constraint(array, pltpu.HBM)
+            for array in (
+                cand_rows.reshape(rows, width),
+                listed.reshape(1, users),
+                block_mask,
+                hist_keys.reshape(hist, width),
+                hist_values.reshape(hist, width),
+                w_query.reshape(depth, width),
+                w_gate.reshape(depth, width),
+                w_out.reshape(depth, width),
+            )
+        ),
         hist_len,
-        block_mask,
-        hist_keys.reshape(hist, width),
-        hist_values.reshape(hist, width),
-        w_query.reshape(depth, width),
-        w_gate.reshape(depth, width),
-        w_out.reshape(depth, width),
     )
     return ranked.reshape(cand_rows.shape)
 

time: 51.1 us -> 48.8 us (0.955)
  Pallas kernels: 49 us -> 47.4 us
  local copies, waits for them, and re-layouts: 1.29 us -> 0.63 us
    pallas_call x1, Pallas kernels: 49 us -> 47.4 us  [on_device(): pl.pallas_call(functools.partial(layer_kernel, caches, ranks, cpr), out_s...]
    unnamed x5 -> x1, local copies, waits for them, and re-layouts: 1.29 us -> 0.63 us
where the time goes in v3:
time: 48.8 us; the launch traced here: 48.7 us
  Pallas kernels  47.4 us (97%)
  between operations  0.66 us (1%)
  local copies, waits for them, and re-layouts  0.63 us (1%)
    pallas_call x1, Pallas kernels, on_device(): pl.pallas_call(functools.partial(layer_kernel, caches, ranks, cpr), out_s...  47.4 us

profile of v3, /device:TPU:1, one launch (start us, length us, event | category | flops | bytes accessed | tf_op | source)
XLA Modules:
  0.0 48.7 jit_solution(8559280063146058552)
XLA Ops:
  0.7 47.4 %hstu_layer.1 = bf16[256,128]{1,0:T(8,128)(2,1)S(1)} custom-call(bf16[256,128]{1,0:T(8,128)(2,1)} %bitcast.14, s32[1,64]{1,0:T(1,128)} %bitcast.15, s32[1,24]{1,0:T(1,128)} %block_mask.1, bf16[3072,128]{1,0:T(8,128)(2,1)} %bitcast.9, bf16[3072,128]{1,0:T(8,128)(2,1)} %bitcast.10, bf16[1024,128]{1,0:T(8,128)(2,1)} %bitcast.11, bf16[1024,128]{1,0:T(8,128)(2,1)} %bitcast.12, ...), custom_call_target="tpu_custom_call" | custom-call | tf_op jit(solution)/shard_map/hstu_layer/pallas_call | solution.py:267
  48.1 0.6 %copy.12 = bf16[1,64,4,128]{3,2,1,0:T(4,128)(2,1)} copy(bf16[1,64,4,128]{3,2,1,0:T(4,128)(2,1)S(1)} %bitcast.8) | data formatting | bytes 131072

commit v4 on v3

--- a/solution.py
+++ b/solution.py
@@ -9,8 +9,9 @@
 
 BLOCK = 128
 EPSILON = 1e-05
-CHUNKS = 2
 PIECES = 4
+GROUPS = ((0, 1), (2, 3))
+CHUNKS = ((0,), (1,))
 KEY_TILE = 1024
 F32 = jnp.float32
 BF16 = jnp.bfloat16
@@ -35,7 +36,6 @@
     my_cache = lax.axis_index("cache")
     my_rank = lax.axis_index("rank")
     rows = caches * cpr
-    part = rows // CHUNKS
     head = keys.shape[1]
     hist = keys.shape[0]
     wide = caches // (2 * DEPTHS)
@@ -150,7 +150,11 @@
     pltpu.make_async_copy(gathered.at[my_rank], gathered.at[my_rank], a_recv).wait()
 
     small = rows // PIECES
-    of_chunk = [range(c * PIECES // CHUNKS, (c + 1) * PIECES // CHUNKS) for c in range(CHUNKS)]
+
+    group_of = {piece: number for number, group in enumerate(GROUPS) for piece in group}
+
+    def span_of(pieces):
+        return pl.ds(pieces[0] * small, len(pieces) * small)
 
     def hop(buffer, phase, piece, slot, step, recv_sem):
         block = buffer.at[rank_at(slot), pl.ds(piece * small, small)]
@@ -163,38 +167,47 @@
             device_id_type=MESH,
         )
 
-    def spread_near(buffer, phase, chunk):
-        for piece in of_chunk[chunk]:
+    def rest(phase, piece):
+        return rest_recv.at[phase, group_of[piece]]
+
+    def spread_near(buffer, phase, pieces):
+        for piece in pieces:
             for way, step in ((0, 2), (1, -2)):
                 hop(buffer, phase, piece, 0, step, near_recv.at[phase, piece, way]).start()
 
-    def spread_next(buffer, phase, chunk):
-        for piece in of_chunk[chunk]:
+    def spread_next(buffer, phase, pieces):
+        for piece in pieces:
             for step in (1, -1):
-                hop(buffer, phase, piece, 0, step, rest_recv.at[phase, chunk]).start()
-
-    def relay(buffer, phase, chunk):
-        for piece in of_chunk[chunk]:
+                hop(buffer, phase, piece, 0, step, rest(phase, piece)).start()
+
+    def relay(buffer, phase, pieces):
+        for piece in pieces:
             for way, step in ((0, 1), (1, -1)):
                 hop(buffer, phase, piece, -2 * step, 2 * step, near_recv.at[phase, piece, way]).wait_recv()
-                hop(buffer, phase, piece, -2 * step, step, rest_recv.at[phase, chunk]).start()
                 if piece % 2 == way:
-                    hop(buffer, phase, piece, -2 * step, 2 * step, rest_recv.at[phase, chunk]).start()
-
-    def complete(buffer, phase, chunk):
-        five = buffer.at[pl.ds(0, 5), pl.ds(chunk * part, part)]
-        pltpu.make_async_copy(five, five, rest_recv.at[phase, chunk]).wait()
-
-    for chunk in range(CHUNKS):
-        spread_near(gathered, 0, chunk)
-    for chunk in range(CHUNKS):
-        spread_next(gathered, 0, chunk)
-    for chunk in range(CHUNKS):
-        relay(gathered, 0, chunk)
-
-    for chunk in range(CHUNKS):
-        complete(gathered, 0, chunk)
-        span = pl.ds(chunk * part, part)
+                    hop(buffer, phase, piece, -2 * step, 2 * step, rest(phase, piece)).start()
+                hop(buffer, phase, piece, -2 * step, step, rest(phase, piece)).start()
+
+    def complete(buffer, phase, group):
+        five = buffer.at[pl.ds(0, 5), span_of(GROUPS[group])]
+        pltpu.make_async_copy(five, five, rest_recv.at[phase, group]).wait()
+
+    def exchange(buffer, phase):
+        every = range(PIECES)
+        spread_next(buffer, phase, every[:-1])
+        relay(buffer, phase, every)
+        spread_next(buffer, phase, every[-1:])
+
+    def pieces_of(chunk):
+        return [piece for group in chunk for piece in GROUPS[group]]
+
+    spread_near(gathered, 0, range(PIECES))
+    exchange(gathered, 0)
+
+    for chunk in CHUNKS:
+        for group in chunk:
+            complete(gathered, 0, group)
+        span = span_of(pieces_of(chunk))
         slices = [gathered[k, span, :].astype(F32) for k in range(ranks)]
         centre = jnp.sum(sum(slices[1:], slices[0]), axis=-1, keepdims=True) * (1.0 / (ranks * head))
         slices = [s - centre for s in slices]
@@ -205,7 +218,7 @@
         both = silu_of_twice(0.5 * jnp.dot(normed, w_in_v[...], preferred_element_type=F32))
         queries = both[:, :head].astype(BF16)
         gate = both[:, head:]
-        attended = jnp.zeros((part, head), F32)
+        attended = jnp.zeros((span.size, head), F32)
         for tile in range(hist // KEY_TILE):
             events = pl.ds(tile * KEY_TILE, KEY_TILE)
             scores = lax.dot_general(
@@ -217,15 +230,13 @@
         attended = attended - centre
         spread_of = jnp.mean(attended * attended, axis=-1, keepdims=True)
         hidden[my_rank, span, :] = (attended * lax.rsqrt(spread_of + EPSILON) * gate).astype(BF16)
-        spread_near(hidden, 1, chunk)
-        spread_next(hidden, 1, chunk)
-
-    for chunk in range(CHUNKS):
-        relay(hidden, 1, chunk)
-
-    for chunk in range(CHUNKS):
-        complete(hidden, 1, chunk)
-        span = pl.ds(chunk * part, part)
+        spread_near(hidden, 1, pieces_of(chunk))
+
+    exchange(hidden, 1)
+
+    for group, pieces in enumerate(GROUPS):
+        complete(hidden, 1, group)
+        span = span_of(pieces)
         whole = jnp.concatenate([hidden[k, span, :] for k in range(ranks)], axis=1)
         projected = jnp.dot(whole, w_out_v[...], preferred_element_type=F32)
         send2[span, :] = (gathered[my_rank, span, :].astype(F32) + projected).astype(BF16)
@@ -240,8 +251,7 @@
                 device_id_type=MESH,
             ).start()
 
-        count = wide // CHUNKS
-        for_depths(FAR_X[chunk * count:(chunk + 1) * count], send_shard)
+        for_depths([FAR_X[piece] for piece in pieces], send_shard)
     pltpu.make_async_copy(send2.at[here], recv2.at[mine], b_recv).start()
 
     pltpu.make_async_copy(recv2, recv2, b_recv).wait()
@@ -287,7 +297,7 @@
             pltpu.SemaphoreType.DMA,
             pltpu.SemaphoreType.DMA,
             pltpu.SemaphoreType.DMA((2, PIECES, 2)),
-            pltpu.SemaphoreType.DMA((2, CHUNKS)),
+            pltpu.SemaphoreType.DMA((2, len(GROUPS))),
             pltpu.SemaphoreType.DMA((2,)),
             pltpu.SemaphoreType.DMA,
             pltpu.SemaphoreType.DMA,

time: 48.8 us -> 48.2 us (0.988)
  Pallas kernels: 47.4 us -> 46.8 us
    pallas_call x1, Pallas kernels: 47.4 us -> 46.8 us  [on_device(): pl.pallas_call(functools.partial(layer_kernel, caches, ranks, cpr), out_s...]
where the time goes in v4:
time: 48.2 us; the launch traced here: 48.1 us
  Pallas kernels  46.8 us (97%)
  between operations  0.66 us (1%)
  local copies, waits for them, and re-layouts  0.63 us (1%)
    pallas_call x1, Pallas kernels, on_device(): pl.pallas_call(functools.partial(layer_kernel, caches, ranks, cpr), out_s...  46.8 us

profile of v4, /device:TPU:1, one launch (start us, length us, event | category | flops | bytes accessed | tf_op | source)
XLA Modules:
  0.0 48.1 jit_solution(14331531276244556209)
XLA Ops:
  0.7 46.8 %hstu_layer.1 = bf16[256,128]{1,0:T(8,128)(2,1)S(1)} custom-call(bf16[256,128]{1,0:T(8,128)(2,1)} %bitcast.14, s32[1,64]{1,0:T(1,128)} %bitcast.15, s32[1,24]{1,0:T(1,128)} %block_mask.1, bf16[3072,128]{1,0:T(8,128)(2,1)} %bitcast.9, bf16[3072,128]{1,0:T(8,128)(2,1)} %bitcast.10, bf16[1024,128]{1,0:T(8,128)(2,1)} %bitcast.11, bf16[1024,128]{1,0:T(8,128)(2,1)} %bitcast.12, ...), custom_call_target="tpu_custom_call" | custom-call | tf_op jit(solution)/shard_map/hstu_layer/pallas_call | solution.py:277
  47.5 0.6 %copy.12 = bf16[1,64,4,128]{3,2,1,0:T(4,128)(2,1)} copy(bf16[1,64,4,128]{3,2,1,0:T(4,128)(2,1)S(1)} %bitcast.8) | data formatting | bytes 131072

commit v5 on v4

--- a/solution.py
+++ b/solution.py
@@ -72,13 +72,8 @@
             barrier, inc=1, device_id={"cache": peer_at(dx, dz, dc)}, device_id_type=MESH
         )
 
-    for_depths(FAR_X, greet)
-
     def rank_at(step):
         return lax.rem(my_rank + (step + ranks), ranks)
-
-    for step in (-2, -1, 1, 2):
-        pl.semaphore_signal(barrier, inc=1, device_id={"rank": rank_at(step)}, device_id_type=MESH)
 
     def load(source, target, number):
         return pltpu.make_async_copy(source, target, load_sem.at[number])
@@ -93,7 +88,13 @@
         load(w_gate, w_in_v.at[:, pl.ds(head, head)], 6),
         load(w_out, w_out_v, 7),
     ]
-    for one in loads:
+
+    for one in loads[:2]:
+        one.start()
+    for_depths(FAR_X, greet)
+    for step in (-2, -1, 1, 2):
+        pl.semaphore_signal(barrier, inc=1, device_id={"rank": rank_at(step)}, device_id_type=MESH)
+    for one in loads[2:]:
         one.start()
 
     users = caches

time: 48.2 us -> 48.2 us (level)
  no operation moved by 1% of the time
where the time goes in v5:
time: 48.2 us; the launch traced here: 48.1 us
  Pallas kernels  46.8 us (97%)
  between operations  0.66 us (1%)
  local copies, waits for them, and re-layouts  0.63 us (1%)
    pallas_call x1, Pallas kernels, on_device(): pl.pallas_call(functools.partial(layer_kernel, caches, ranks, cpr), out_s...  46.8 us

profile of v5, /device:TPU:1, one launch (start us, length us, event | category | flops | bytes accessed | tf_op | source)
XLA Modules:
  0.0 48.1 jit_solution(2242526327722886533)
XLA Ops:
  0.7 46.8 %hstu_layer.1 = bf16[256,128]{1,0:T(8,128)(2,1)S(1)} custom-call(bf16[256,128]{1,0:T(8,128)(2,1)} %bitcast.14, s32[1,64]{1,0:T(1,128)} %bitcast.15, s32[1,24]{1,0:T(1,128)} %block_mask.1, bf16[3072,128]{1,0:T(8,128)(2,1)} %bitcast.9, bf16[3072,128]{1,0:T(8,128)(2,1)} %bitcast.10, bf16[1024,128]{1,0:T(8,128)(2,1)} %bitcast.11, bf16[1024,128]{1,0:T(8,128)(2,1)} %bitcast.12, ...), custom_call_target="tpu_custom_call" | custom-call | tf_op jit(solution)/shard_map/hstu_layer/pallas_call | solution.py:278
  47.5 0.6 %copy.12 = bf16[1,64,4,128]{3,2,1,0:T(4,128)(2,1)} copy(bf16[1,64,4,128]{3,2,1,0:T(4,128)(2,1)S(1)} %bitcast.8) | data formatting | bytes 131072

commit v6 on v5

--- a/solution.py
+++ b/solution.py
@@ -10,8 +10,8 @@
 BLOCK = 128
 EPSILON = 1e-05
 PIECES = 4
-GROUPS = ((0, 1), (2, 3))
-CHUNKS = ((0,), (1,))
+GROUPS = ((0, 1), (2,), (3,))
+CHUNKS = ((0,), (1, 2))
 KEY_TILE = 1024
 F32 = jnp.float32
 BF16 = jnp.bfloat16
@@ -45,9 +45,11 @@
 
     barrier = pltpu.get_barrier_semaphore()
 
+    wide_part = [lax.rem(my_x + dx, wide) * (2 * DEPTHS) for dx in range(wide)]
+    core_part = [my_core, 1 - my_core]
+
     def peer_at(dx, dz, dc):
-        x, z, core = lax.rem(my_x + dx, wide), lax.rem(my_z + dz, DEPTHS), lax.rem(my_core + dc, 2)
-        return (x * DEPTHS + z) * 2 + core
+        return wide_part[dx] + core_part[dc] + lax.rem(my_z + dz, DEPTHS) * 2
 
     def back(step, extent):
         return (extent - step) % extent if isinstance(step, int) else lax.rem(extent - step, extent)
@@ -69,11 +71,13 @@
 
     def greet(dx, dz, dc):
         pl.semaphore_signal(
-            barrier, inc=1, device_id={"cache": peer_at(dx, dz, dc)}, device_id_type=MESH
+            barrier, inc=1, device_id=(peer_at(dx, dz, dc), my_rank), device_id_type=MESH
         )
 
+    rank_part = [lax.rem(my_rank + step, ranks) for step in range(ranks)]
+
     def rank_at(step):
-        return lax.rem(my_rank + (step + ranks), ranks)
+        return rank_part[step % ranks]
 
     def load(source, target, number):
         return pltpu.make_async_copy(source, target, load_sem.at[number])
@@ -93,7 +97,7 @@
         one.start()
     for_depths(FAR_X, greet)
     for step in (-2, -1, 1, 2):
-        pl.semaphore_signal(barrier, inc=1, device_id={"rank": rank_at(step)}, device_id_type=MESH)
+        pl.semaphore_signal(barrier, inc=1, device_id=(my_cache, rank_at(step)), device_id_type=MESH)
     for one in loads[2:]:
         one.start()
 
@@ -129,7 +133,7 @@
             dst_ref=gathered.at[my_rank, of_place(back(dx, wide), back(dz, DEPTHS), dc)],
             send_sem=a_send,
             recv_sem=a_recv,
-            device_id={"cache": peer},
+            device_id=(peer, my_rank),
             device_id_type=MESH,
         ).start()
 
@@ -164,7 +168,7 @@
             dst_ref=block,
             send_sem=ring_send.at[phase],
             recv_sem=recv_sem,
-            device_id={"rank": rank_at(step)},
+            device_id=(my_cache, rank_at(step)),
             device_id_type=MESH,
         )
 
@@ -248,7 +252,7 @@
                 dst_ref=recv2.at[mine],
                 send_sem=b_send,
                 recv_sem=b_recv,
-                device_id={"cache": peer_at(dx, dz, dc)},
+                device_id=(peer_at(dx, dz, dc), my_rank),
                 device_id_type=MESH,
             ).start()
 

time: 48.2 us -> 48.2 us (level)
  no operation moved by 1% of the time
where the time goes in v6:
time: 48.2 us; the launch traced here: 48.1 us
  Pallas kernels  46.8 us (97%)
  between operations  0.66 us (1%)
  local copies, waits for them, and re-layouts  0.63 us (1%)
    pallas_call x1, Pallas kernels, on_device(): pl.pallas_call(functools.partial(layer_kernel, caches, ranks, cpr), out_s...  46.8 us

profile of v6, /device:TPU:1, one launch (start us, length us, event | category | flops | bytes accessed | tf_op | source)
XLA Modules:
  0.0 48.1 jit_solution(7075419398766161434)
XLA Ops:
  0.7 46.8 %hstu_layer.1 = bf16[256,128]{1,0:T(8,128)(2,1)S(1)} custom-call(bf16[256,128]{1,0:T(8,128)(2,1)} %bitcast.14, s32[1,64]{1,0:T(1,128)} %bitcast.15, s32[1,24]{1,0:T(1,128)} %block_mask.1, bf16[3072,128]{1,0:T(8,128)(2,1)} %bitcast.9, bf16[3072,128]{1,0:T(8,128)(2,1)} %bitcast.10, bf16[1024,128]{1,0:T(8,128)(2,1)} %bitcast.11, bf16[1024,128]{1,0:T(8,128)(2,1)} %bitcast.12, ...), custom_call_target="tpu_custom_call" | custom-call | tf_op jit(solution)/shard_map/hstu_layer/pallas_call | solution.py:282
  47.5 0.6 %copy.12 = bf16[1,64,4,128]{3,2,1,0:T(4,128)(2,1)} copy(bf16[1,64,4,128]{3,2,1,0:T(4,128)(2,1)S(1)} %bitcast.8) | data formatting | bytes 131072
